TPU v7x, 256 devices: a whole 4x4x8 slice. The times are simulated.
256 devices in a mesh: req: 32 (over x, y, core), exp: 8 (over z).
Axes of the slice: x: 4, y: 4, z: 8, core: 2. Of those that a mesh axis runs over, the one named last changes fastest.
Arguments:
- residual: bfloat16 [4096, 2048], P(('req', 'exp')), may hold values from -12 to 12
- queries: bfloat16 [4096, 2, 2048], P('req', None, 'exp'), may hold values from -9 to 9
- kv_cache: bfloat16 [608, 2, 128, 2048], P('req', None, None, 'exp'), may hold values from -4 to 4
- page_table: int32 [288, 11], P('req'), may hold values from 0 to 18, as said below
- seq_lengths: int32 [288], P('req'), may hold values from 8 to 1408, as said below
- head_route: int32 [4096, 2], P('req'), may hold values from 0 to 7, all different within a row
- head_gate: float32 [4096, 2], P('req'), may hold values from 0.2 to 1
- out_weight: bfloat16 [8, 2048, 2048], P(None, 'exp'), may hold values from -0.5 to 0.5
- norm_gain: float32 [2048], replicated, may hold values from 0.25 to 1.75
- expert_route: int32 [4096, 2], P(('req', 'exp')), may hold values from 0 to 7, all different within a row; in each aligned block of 16 rows (0 to 15, 16 to 31, ...) at most 8 rows name the same one
- expert_gate: float32 [4096, 2], P(('req', 'exp')), may hold values from 0.2 to 1
- gate_up: bfloat16 [8, 2, 2048, 5632], P('exp', None, None, 'req'), may hold values from -0.125 to 0.125
- down_weight: bfloat16 [8, 5632, 2048], P('exp', 'req'), may hold values from -0.078125 to 0.078125
Outputs:
- attended: bfloat16 [4096, 2048], P(('req', 'exp'))
- expert_mix: bfloat16 [4096, 2048], P(('req', 'exp'))
Inputs may be any that keep to these rules, and one draw needn't show every extreme that they name: `page_table`: pages are numbered within the slot's group. A group's slot 0 lists 11 different pages; each other slot repeats one page along its row; no two slots of a group share a page. `seq_lengths`: slot 0 of every group is a prefill request of length at least 120; the other slots are decode requests of length at most 128. `head_route`: each row names 2 different attention experts. `expert_route`: each row names 2 different experts; within the rows of one device no expert is named by more than 8 rows.
All inputs are finite; a program needn't handle non-finite values.
Results may differ from a plain program's by a relative error of at most 0.023.
Values may be sent and summed in bfloat16 or wider, within the bound.
A program may use at most 128 MiB of HBM per device.

v0:
```python
import jax
import jax.numpy as jnp
from jax import lax
from jax.sharding import PartitionSpec as P

HD = 128
TOPA = 2
SPAN = 120


def attend_local(queries_one, key_rows, value_rows, positions, head_count):
    amount = queries_one.shape[0]
    heads_q = queries_one.reshape(amount * TOPA, head_count, HD)
    heads_k = key_rows.reshape(-1, head_count, HD)
    heads_v = value_rows.reshape(-1, head_count, HD)
    scores = jnp.einsum(
        "qhd,khd->hqk", heads_q, heads_k, preferred_element_type=jnp.float32
    ) * HD ** (-0.5)
    key_pos = jnp.arange(heads_k.shape[0], dtype=jnp.int32)
    row_pos = jnp.repeat(positions, TOPA)
    allowed = key_pos[None, :] <= row_pos[:, None]
    scores = jnp.where(allowed[None], scores, -1e30)
    row_max = jnp.max(scores, axis=2, keepdims=True)
    raised = jnp.exp(scores - row_max)
    attention_weights = (raised / jnp.sum(raised, axis=2, keepdims=True)).astype(jnp.bfloat16)
    mixture = jnp.einsum(
        "hqk,khd->qhd", attention_weights, heads_v, preferred_element_type=jnp.float32
    )
    return mixture.astype(jnp.bfloat16).reshape(amount, TOPA, head_count * HD)


def local(
    residual,
    queries,
    kv_cache,
    page_table,
    seq_lengths,
    head_route,
    head_gate,
    out_weight,
    norm_gain,
    expert_route,
    expert_gate,
    gate_up,
    down_weight,
):
    feature_width = queries.shape[2]
    head_count = feature_width // HD
    page_rows = kv_cache[page_table[0]]
    key_rows = page_rows[:, 0].reshape(-1, feature_width)
    value_rows = page_rows[:, 1].reshape(-1, feature_width)
    prefill_pos = seq_lengths[0] - SPAN + jnp.arange(SPAN, dtype=jnp.int32)
    prefill_out = attend_local(queries[:SPAN], key_rows, value_rows, prefill_pos, head_count)
    decode_pages = kv_cache[page_table[1:, 0]]

    def decode_one(query_row, page_block, length):
        return attend_local(
            query_row[None], page_block[0], page_block[1], (length - 1)[None], head_count
        )[0]

    decode_out = jax.vmap(decode_one)(queries[SPAN:], decode_pages, seq_lengths[1:])
    mixture = jnp.concatenate([prefill_out, decode_out], axis=0)
    partial_value = jnp.zeros((mixture.shape[0], residual.shape[1]), jnp.float32)
    for expert_index in range(out_weight.shape[0]):
        picked = head_route == expert_index
        chosen = jnp.sum(jnp.where(picked[:, :, None], mixture, jnp.zeros_like(mixture)), axis=1)
        weight = jnp.sum(jnp.where(picked, head_gate, jnp.zeros_like(head_gate)), axis=1)
        partial_value = partial_value + weight[:, None] * jnp.dot(
            chosen, out_weight[expert_index], preferred_element_type=jnp.float32
        )
    row_count = residual.shape[0]
    summed = lax.psum(partial_value.astype(jnp.bfloat16), "exp").astype(jnp.float32)
    own_heads = lax.dynamic_slice_in_dim(summed, lax.axis_index("exp") * row_count, row_count, 0)
    attended = (residual.astype(jnp.float32) + own_heads).astype(jnp.bfloat16)
    values_f = attended.astype(jnp.float32)
    normed = (
        values_f
        * lax.rsqrt(jnp.mean(values_f * values_f, axis=1, keepdims=True) + 1e-06)
        * norm_gain
    ).astype(jnp.bfloat16)
    experts = lax.axis_size("exp")
    capacity = max(2, 2 * TOPA * row_count // experts)
    flat_route = expert_route.reshape(-1)
    onehot = (flat_route[:, None] == jnp.arange(experts, dtype=jnp.int32)[None, :]).astype(
        jnp.int32
    )
    earlier = jnp.cumsum(onehot, axis=0) - onehot
    rank_index = jnp.sum(earlier * onehot, axis=1)
    slot_index = flat_route * capacity + rank_index
    placing = (
        jnp.arange(experts * capacity, dtype=jnp.int32)[:, None] == slot_index[None, :]
    ).astype(jnp.bfloat16)
    repeated = jnp.repeat(normed, TOPA, axis=0)
    outgoing = jnp.dot(placing, repeated, preferred_element_type=jnp.float32).astype(jnp.bfloat16)
    w_gate = gate_up[0, 0]
    w_up = gate_up[0, 1]
    w_down = down_weight[0]
    arrived = lax.all_to_all(outgoing, "exp", split_axis=0, concat_axis=0, tiled=True)
    portion = lax.all_gather(arrived, "req", axis=0, tiled=True)
    gate_part = jnp.dot(portion, w_gate, preferred_element_type=jnp.float32)
    up_part = jnp.dot(portion, w_up, preferred_element_type=jnp.float32)
    active = (jax.nn.silu(gate_part) * up_part).astype(jnp.bfloat16)
    portion = active
    returned = lax.psum_scatter(
        jnp.dot(portion, w_down, preferred_element_type=jnp.float32).astype(jnp.bfloat16),
        "req",
        scatter_dimension=0,
        tiled=True,
    )
    homeward = lax.all_to_all(returned, "exp", split_axis=0, concat_axis=0, tiled=True)
    picked_rows = jnp.take(homeward, slot_index, axis=0).astype(jnp.float32)
    weighted = picked_rows * expert_gate.reshape(-1)[:, None]
    expert_mix = jnp.sum(weighted.reshape(row_count, TOPA, -1), axis=1).astype(jnp.bfloat16)
    return (attended, expert_mix)


def solution(mesh):
    return jax.shard_map(
        local,
        mesh=mesh,
        in_specs=(
            P(("req", "exp"), None),
            P("req", None, "exp"),
            P("req", None, None, "exp"),
            P("req", None),
            P("req"),
            P("req", None),
            P("req", None),
            P(None, "exp", None),
            P(),
            P(("req", "exp"), None),
            P(("req", "exp"), None),
            P("exp", None, None, "req"),
            P("exp", "req", None),
        ),
        out_specs=(P(("req", "exp"), None), P(("req", "exp"), None)),
        check_vma=False,
    )
```

profile of v0, /device:TPU:2, one launch (start us, length us, event | category | flops | bytes accessed | tf_op | source)
XLA Modules:
  0.0 351.9 jit_solution(16315062266536121598)
XLA Ops:
  8.9 1.3 select_reduce_fusion.1
  15.4 1.8 gather_fusion
  17.2 2.4 fusion.83
  19.6 2.6 reshape_reshape_squeeze.7
  25.2 3.9 %fusion.86 = (f32[2,240]{1,0:T(2,128)S(1)}, f32[2,240,1408]{2,1,0:T(8,128)}) fusion(pred[240,1408]{1,0:T(8,128)(4,1)} %iota_compare_fusion, bf16[1408,2,128]{2,1,0:T(2,128)(2,1)} %reshape_reshape_squeeze.7, bf16[240,2,128]{2,1,0:T(2,128)(2,1)S(1)} %reshape.164), kind=kOutput, calls=%fused_computation.145 | convolution fusion | flops 175719808 | bytes 3886976 | tf_op jit(solution)/shard_map/sub | solution.py:24
  29.0 2.4 fusion.18
  38.5 2.2 fusion.85
  41.9 3.8 %fusion.63 = (bf16[128,256]{1,0:T(8,128)(2,1)S(1)}, bf16[128,256]{1,0:T(8,128)(2,1)S(1)}, bf16[128,256]{1,0:T(8,128)(2,1)S(1)}, bf16[128,256]{1,0:T(8,128)(2,1)S...) fusion(pred[128,2]{1,0:T(8,128)(4,1)} %copy.77, ...), kind=kLoop, calls=%fused_computation.90 | loop fusion | flops 851968 | bytes 657408 | tf_op jit(solution)/shard_map/reduce_sum | solution.py:66
  45.7 1.5 convolution_multiply_fusion.9
  47.3 1.5 fusion.13
  48.9 1.5 fusion.12
  50.4 1.5 fusion.11
  52.0 1.5 fusion.10
  53.6 1.5 fusion.9
  55.2 1.6 fusion.8
  56.7 2.4 fusion.14
  59.7 76.3 %all-reduce.2.cloned.1.call-done = bf16[128,2048]{1,0:T(8,128)(2,1)} async-done(((bf16[128,2048]{1,0:T(8,128)(2,1)}), bf16[128,2048]{1,0:T(8,128)(2,1)}) %all-reduce.2.cloned.1.call-update) | async-done | bytes 524304 | tf_op jit(solution)/shard_map/psum | solution.py:72
  137.4 14.4 %all_to_all.24 = bf16[8,8,2048]{2,1,0:T(8,128)(2,1)} all-to-all(bf16[8,8,2048]{2,1,0:T(8,128)(2,1)S(1)} %fusion.15), channel_id=1, replica_groups=mesh['req'=32,'exp'=8] {'exp'}, dimensions={0} | all-to-all | bytes 524288 | tf_op jit(solution)/shard_map/all_to_all | solution.py:98
  152.1 53.8 %all-gather.2.cloned.1.call-done = bf16[2048,2048]{1,0:T(8,128)(2,1)} async-done(((bf16[64,2048]{1,0:T(8,128)(2,1)}), bf16[2048,2048]{1,0:T(8,128)(2,1)}) %all-gather.2.cloned.1.call-update) | async-done | bytes 8388624 | tf_op jit(solution)/shard_map/all_gather | solution.py:99
  205.9 7.5 %fusion.43 = f32[2048,176]{0,1:T(8,128)} fusion(bf16[2048,2048]{1,0:T(8,128)(2,1)} %all-gather.2.cloned.1.call-done, bf16[1,2,2048,176]{2,3,1,0:T(8,128)(2,1)} %param.24), kind=kOutput, calls=%fused_computation.61 | convolution fusion | flops 1476395008 | bytes 10551296 | tf_op jit(solution)/shard_map/dot_general | solution.py:100
  213.5 12.5 %convolution_convert_fusion = bf16[2048,2048]{1,0:T(8,128)(2,1)} fusion(bf16[2048,2048]{1,0:T(8,128)(2,1)} %all-gather.2.cloned.1.call-done, f32[2048,176]{0,1:T(8,128)} %fusion.43, bf16[1,176,2048]{2,1,0:T(8,128)(2,1)} %param.25, bf16[1,2,2048,176]{2,3,1,0:T(8,128)(2,1)} %param.24), kind=kOutput, calls=%fused_computation.5 | convolution fusion | flops 2959147008 | bytes 19660800 | tf_op jit(solution)/shard_map/dot_general | solution.py:105
  226.4 99.6 %reduce-scatter.2.cloned.1.call-done = bf16[64,2048]{1,0:T(8,128)(2,1)} async-done(((bf16[2048,2048]{1,0:T(8,128)(2,1)}), bf16[64,2048]{1,0:T(8,128)(2,1)}) %reduce-scatter.2.cloned.1.call-update) | async-done | bytes 262160 | tf_op jit(solution)/shard_map/reduce_scatter | solution.py:104
  326.0 7.0 %all-to-all-start.1 = ((bf16[8,8,2048]{2,1,0:T(8,128)(2,1)}), bf16[8,8,2048]{2,1,0:T(8,128)(2,1)S(1)}, u32[]{:S(2)}, u32[]{:S(2)}) async-start(bf16[8,8,2048]{2,1,0:T(8,128)(2,1)} %bitcast.101), calls=%async_computation.2 | async-start | bytes 524288 | tf_op jit(solution)/shard_map/all_to_all | solution.py:110
  333.2 10.3 %all-to-all-done.1 = bf16[8,8,2048]{2,1,0:T(8,128)(2,1)S(1)} async-done(((bf16[8,8,2048]{2,1,0:T(8,128)(2,1)}), bf16[8,8,2048]{2,1,0:T(8,128)(2,1)S(1)}, u32[]{:S(2)}, u32[]{:S(2)}) %all-to-all-start.1) | async-done | bytes 262176 | tf_op jit(solution)/shard_map/all_to_all | solution.py:110
  (90 shorter events, 22.8 us)
Async XLA Ops:
  7.2 8.2 %copy-start = (bf16[19,2,128,256]{3,2,1,0:T(8,128)(2,1)S(1)}, bf16[19,2,128,256]{3,2,1,0:T(8,128)(2,1)}, u32[]{:S(2)}) copy-start(bf16[19,2,128,256]{3,2,1,0:T(8,128)(2,1)} %param.15) | copy-start | bytes 7471108
  7.2 128.8 %all-reduce.2.cloned.1.call-start = ((), (), s32[]{:S(2)}) async-start(), calls=%async_computation.3 | async-start | bytes 1048576 | tf_op jit(solution)/shard_map/psum | solution.py:72
  17.2 5.0 %copy-start.14 = (s32[9]{0:T(128)S(1)}, s32[9]{0:T(128)}, u32[]{:S(2)}) copy-start(s32[9]{0:T(128)} %param.17) | copy-start | bytes 112
  17.2 6.8 %slice-start = ((bf16[128,2,256]{2,1,0:T(2,128)(2,1)}), bf16[120,2,256]{2,1,0:T(2,128)(2,1)S(1)}, s32[]{:S(2)}) async-start(bf16[128,2,256]{2,1,0:T(2,128)(2,1)} %param.14), calls=%async_computation.6 | async-start | bytes 245760 | tf_op jit(solution)/shard_map/slice | solution.py:53
  25.2 3.9 %copy-start.1 = (bf16[1408,2,128]{2,1,0:T(2,128)(2,1)S(1)}, bf16[1408,2,128]{2,1,0:T(2,128)(2,1)}, u32[]{:S(2)}) copy-start(bf16[1408,2,128]{2,1,0:T(2,128)(2,1)} %reshape_reshape_squeeze.6) | copy-start | bytes 2162692
  40.8 6.5 %copy-start.12 = (f32[128]{0:T(128)S(1)}, f32[128]{0:T(128)}, u32[]{:S(2)}) copy-start(f32[128]{0:T(128)} %get-tuple-element.15) | copy-start | bytes 1540
  45.7 3.1 copy-start.11
  47.3 3.1 copy-start.10
  48.9 3.1 copy-start.9
  50.4 3.1 copy-start.8
  52.0 3.1 copy-start.7
  53.6 3.2 copy-start.6
  55.1 4.1 %copy-start.4 = (s32[16,2]{0,1:T(2,128)S(1)}, s32[16,2]{0,1:T(2,128)}, u32[]{:S(2)}) copy-start(s32[16,2]{0,1:T(2,128)} %param.22) | copy-start | bytes 388
  55.1 80.8 %copy-start.3 = (bf16[16,2048]{1,0:T(8,128)(2,1)S(1)}, bf16[16,2048]{1,0:T(8,128)(2,1)}, u32[]{:S(2)}) copy-start(bf16[16,2048]{1,0:T(8,128)(2,1)} %param.13) | copy-start | bytes 196612
  55.1 81.8 %copy-start.5 = (f32[2048]{0:T(1024)S(1)}, f32[2048]{0:T(1024)}, u32[]{:S(2)}) copy-start(f32[2048]{0:T(1024)} %param.21) | copy-start | bytes 24580
  59.1 146.8 %all-gather.2.cloned.1.call-start = ((), (), s32[]{:S(2)}) async-start(), calls=%async_computation.4 | async-start | bytes 8650752 | tf_op jit(solution)/shard_map/all_gather | solution.py:99
  137.0 76.5 %copy-start.2 = (bf16[16,2048]{1,0:T(8,128)(2,1)}, bf16[16,2048]{1,0:T(8,128)(2,1)S(1)}, u32[]{:S(2)}) copy-start(bf16[16,2048]{1,0:T(8,128)(2,1)S(1)} %get-tuple-element.19) | copy-start | bytes 196612
  151.9 174.1 %reduce-scatter.2.cloned.1.call-start = ((), (), s32[]{:S(2)}) async-start(), calls=%async_computation.5 | async-start | bytes 8650752 | tf_op jit(solution)/shard_map/reduce_scatter | solution.py:104
  226.0 107.1 %copy-start.13 = (f32[16,2]{0,1:T(2,128)S(1)}, f32[16,2]{0,1:T(2,128)}, u32[]{:S(2)}) copy-start(f32[16,2]{0,1:T(2,128)} %param.23) | copy-start | bytes 388
  326.0 17.5 %all-to-all-start.1 = ((bf16[8,8,2048]{2,1,0:T(8,128)(2,1)}), bf16[8,8,2048]{2,1,0:T(8,128)(2,1)S(1)}, u32[]{:S(2)}, u32[]{:S(2)}) async-start(bf16[8,8,2048]{2,1,0:T(8,128)(2,1)} %bitcast.101), calls=%async_computation.2 | async-start | bytes 524288 | tf_op jit(solution)/shard_map/all_to_all | solution.py:110
Sparse Core Ops, SparseCore 0:
  59.2 76.6 all-reduce.1
  152.0 53.8 all-gather.1
  226.2 99.7 reduce-scatter.1
where the time goes:
time: 353 us; the launch traced here: 352 us
  waiting for transfers between devices  240 us (68%)
  matrix products  43 us (12%)
  local copies, waits for them, and re-layouts  20.2 us (6%)
  blocking collectives  14.4 us (4%)
  between operations  14.1 us (4%)
  other arithmetic  12.8 us (4%)
  starting transfers between devices  7.29 us (2%)
    reduce_scatter x1, waiting for transfers between devices, local(): lax.psum_scatter(jnp.dot(portion, w_down, preferred_element_type=jnp.floa...  99.6 us
    psum x1, waiting for transfers between devices, local(): lax.psum(partial_value.astype(jnp.bfloat16), 'exp').astype(jnp.float32)  76.3 us
    all_gather x1, waiting for transfers between devices, local(): portion = lax.all_gather(arrived, 'req', axis=0, tiled=True)  53.8 us
    all_to_all x1, blocking collectives, local(): lax.all_to_all(outgoing, 'exp', split_axis=0, concat_axis=0, tiled=True)  14.4 us
    dot_general x8, matrix products, local(): jnp.dot(chosen, out_weight[expert_index], preferred_element_type=jnp.floa...  13.1 us
    dot_general x1, matrix products, local(): jnp.dot(portion, w_down, preferred_element_type=jnp.float32)  12.5 us
    all_to_all x1, waiting for transfers between devices, local(): lax.all_to_all(returned, 'exp', split_axis=0, concat_axis=0, tiled=True)  10.3 us
    dot_general x1, matrix products, local(): gate_part = jnp.dot(portion, w_gate, preferred_element_type=jnp.float32)  7.55 us
  transfers between devices with their start and end apart: 4, of which 4 were waited for; matrix products, arithmetic and copies ran while one was open for 0% of the time, Pallas kernels for 0%

commit v1 on v0

--- a/solution.py
+++ b/solution.py
@@ -6,6 +6,10 @@
 HD = 128
 TOPA = 2
 SPAN = 120
+
+
+def order_arrays(payload, axis_key):
+    return lax.all_gather(payload, axis_key).sum(axis=0)
 
 
 def attend_local(queries_one, key_rows, value_rows, positions, head_count):
@@ -69,7 +73,7 @@
             chosen, out_weight[expert_index], preferred_element_type=jnp.float32
         )
     row_count = residual.shape[0]
-    summed = lax.psum(partial_value.astype(jnp.bfloat16), "exp").astype(jnp.float32)
+    summed = order_arrays(partial_value.astype(jnp.bfloat16), "exp").astype(jnp.float32)
     own_heads = lax.dynamic_slice_in_dim(summed, lax.axis_index("exp") * row_count, row_count, 0)
     attended = (residual.astype(jnp.float32) + own_heads).astype(jnp.bfloat16)
     values_f = attended.astype(jnp.float32)

time: 353 us -> 338 us (0.958)
  waiting for transfers between devices: 240 us -> 221 us
    psum x1 -> x0, waiting for transfers between devices: 76.3 us -> none  [local(): lax.psum(partial_value.astype(jnp.bfloat16), 'exp').astype(jnp.float32)]
    all_gather x0 -> x1, waiting for transfers between devices: none -> 57.3 us  [order_arrays(): return lax.all_gather(payload, axis_key).sum(axis=0)]
where the time goes in v1:
time: 338 us; the launch traced here: 337 us
  waiting for transfers between devices  221 us (65%)
  matrix products  43 us (13%)
  local copies, waits for them, and re-layouts  20.2 us (6%)
  blocking collectives  15.9 us (5%)
  other arithmetic  15 us (4%)
  between operations  14.1 us (4%)
  starting transfers between devices  7.35 us (2%)
    reduce_scatter x1, waiting for transfers between devices, local(): lax.psum_scatter(jnp.dot(portion, w_down, preferred_element_type=jnp.floa...  99.6 us
    all_gather x1, waiting for transfers between devices, order_arrays(): return lax.all_gather(payload, axis_key).sum(axis=0)  57.3 us
    all_gather x1, waiting for transfers between devices, local(): portion = lax.all_gather(arrived, 'req', axis=0, tiled=True)  53.8 us
    all_to_all x1, blocking collectives, local(): lax.all_to_all(outgoing, 'exp', split_axis=0, concat_axis=0, tiled=True)  15.9 us
    dot_general x8, matrix products, local(): jnp.dot(chosen, out_weight[expert_index], preferred_element_type=jnp.floa...  13.1 us
    dot_general x1, matrix products, local(): jnp.dot(portion, w_down, preferred_element_type=jnp.float32)  12.5 us
    all_to_all x1, waiting for transfers between devices, local(): lax.all_to_all(returned, 'exp', split_axis=0, concat_axis=0, tiled=True)  10.3 us
    dot_general x1, matrix products, local(): gate_part = jnp.dot(portion, w_gate, preferred_element_type=jnp.float32)  7.55 us
  transfers between devices with their start and end apart: 4, of which 4 were waited for; matrix products, arithmetic and copies ran while one was open for 0% of the time, Pallas kernels for 0%

profile of v1, /device:TPU:2, one launch (start us, length us, event | category | flops | bytes accessed | tf_op | source)
XLA Modules:
  0.0 336.5 jit_solution(1039703793063086567)
XLA Ops:
  15.4 1.8 gather_fusion
  17.2 2.4 fusion.83
  19.6 2.6 reshape_reshape_squeeze.7
  25.2 3.9 %fusion.86 = (f32[2,240]{1,0:T(2,128)S(1)}, f32[2,240,1408]{2,1,0:T(8,128)}) fusion(pred[240,1408]{1,0:T(8,128)(4,1)} %iota_compare_fusion, bf16[1408,2,128]{2,1,0:T(2,128)(2,1)} %reshape_reshape_squeeze.7, bf16[240,2,128]{2,1,0:T(2,128)(2,1)S(1)} %reshape.164), kind=kOutput, calls=%fused_computation.145 | convolution fusion | flops 175719808 | bytes 3886976 | tf_op jit(solution)/shard_map/sub | solution.py:28
  29.0 2.4 fusion.18
  38.5 2.2 fusion.85
  41.9 3.8 %fusion.63 = (bf16[128,256]{1,0:T(8,128)(2,1)S(1)}, bf16[128,256]{1,0:T(8,128)(2,1)S(1)}, bf16[128,256]{1,0:T(8,128)(2,1)S(1)}, bf16[128,256]{1,0:T(8,128)(2,1)S...) fusion(pred[128,2]{1,0:T(8,128)(4,1)} %copy.77, ...), kind=kLoop, calls=%fused_computation.90 | loop fusion | flops 851968 | bytes 657408 | tf_op jit(solution)/shard_map/reduce_sum | solution.py:70
  45.7 1.5 convolution_multiply_fusion.9
  47.3 1.5 fusion.13
  48.9 1.5 fusion.12
  50.4 1.5 fusion.11
  52.0 1.5 fusion.10
  53.6 1.5 fusion.9
  55.1 1.5 fusion.8
  56.7 2.3 fusion.14
  59.6 57.3 %all-gather.6.cloned.1.call-done = bf16[1024,2048]{1,0:T(8,128)(2,1)} async-done(((bf16[128,2048]{1,0:T(8,128)(2,1)}), bf16[1024,2048]{1,0:T(8,128)(2,1)}) %all-gather.6.cloned.1.call-update) | async-done | bytes 4194320 | tf_op jit(solution)/shard_map/all_gather | solution.py:12
  116.9 3.0 reduce_sum.247
  120.5 15.9 %all_to_all.24 = bf16[8,8,2048]{2,1,0:T(8,128)(2,1)} all-to-all(bf16[8,8,2048]{2,1,0:T(8,128)(2,1)S(1)} %fusion.15), channel_id=1, replica_groups=mesh['req'=32,'exp'=8] {'exp'}, dimensions={0} | all-to-all | bytes 524288 | tf_op jit(solution)/shard_map/all_to_all | solution.py:102
  136.7 53.8 %all-gather.4.cloned.1.call-done = bf16[2048,2048]{1,0:T(8,128)(2,1)} async-done(((bf16[64,2048]{1,0:T(8,128)(2,1)}), bf16[2048,2048]{1,0:T(8,128)(2,1)}) %all-gather.4.cloned.1.call-update) | async-done | bytes 8388624 | tf_op jit(solution)/shard_map/all_gather | solution.py:103
  190.5 7.5 %fusion.43 = f32[2048,176]{0,1:T(8,128)} fusion(bf16[2048,2048]{1,0:T(8,128)(2,1)} %all-gather.4.cloned.1.call-done, bf16[1,2,2048,176]{2,3,1,0:T(8,128)(2,1)} %param.24), kind=kOutput, calls=%fused_computation.61 | convolution fusion | flops 1476395008 | bytes 10551296 | tf_op jit(solution)/shard_map/dot_general | solution.py:104
  198.1 12.5 %convolution_convert_fusion = bf16[2048,2048]{1,0:T(8,128)(2,1)} fusion(bf16[2048,2048]{1,0:T(8,128)(2,1)} %all-gather.4.cloned.1.call-done, f32[2048,176]{0,1:T(8,128)} %fusion.43, bf16[1,176,2048]{2,1,0:T(8,128)(2,1)} %param.25, bf16[1,2,2048,176]{2,3,1,0:T(8,128)(2,1)} %param.24), kind=kOutput, calls=%fused_computation.5 | convolution fusion | flops 2959147008 | bytes 19660800 | tf_op jit(solution)/shard_map/dot_general | solution.py:109
  211.0 99.6 %reduce-scatter.2.cloned.1.call-done = bf16[64,2048]{1,0:T(8,128)(2,1)} async-done(((bf16[2048,2048]{1,0:T(8,128)(2,1)}), bf16[64,2048]{1,0:T(8,128)(2,1)}) %reduce-scatter.2.cloned.1.call-update) | async-done | bytes 262160 | tf_op jit(solution)/shard_map/reduce_scatter | solution.py:108
  310.5 7.0 %all-to-all-start.1 = ((bf16[8,8,2048]{2,1,0:T(8,128)(2,1)}), bf16[8,8,2048]{2,1,0:T(8,128)(2,1)S(1)}, u32[]{:S(2)}, u32[]{:S(2)}) async-start(bf16[8,8,2048]{2,1,0:T(8,128)(2,1)} %bitcast.103), calls=%async_computation.2 | async-start | bytes 524288 | tf_op jit(solution)/shard_map/all_to_all | solution.py:114
  317.8 10.3 %all-to-all-done.1 = bf16[8,8,2048]{2,1,0:T(8,128)(2,1)S(1)} async-done(((bf16[8,8,2048]{2,1,0:T(8,128)(2,1)}), bf16[8,8,2048]{2,1,0:T(8,128)(2,1)S(1)}, u32[]{:S(2)}, u32[]{:S(2)}) %all-to-all-start.1) | async-done | bytes 262176 | tf_op jit(solution)/shard_map/all_to_all | solution.py:114
  (91 shorter events, 23.3 us)
Async XLA Ops:
  7.2 8.2 %copy-start = (bf16[19,2,128,256]{3,2,1,0:T(8,128)(2,1)S(1)}, bf16[19,2,128,256]{3,2,1,0:T(8,128)(2,1)}, u32[]{:S(2)}) copy-start(bf16[19,2,128,256]{3,2,1,0:T(8,128)(2,1)} %param.15) | copy-start | bytes 7471108
  7.2 109.7 %all-gather.6.cloned.1.call-start = ((), (), s32[]{:S(2)}) async-start(), calls=%async_computation.5 | async-start | bytes 4718592 | tf_op jit(solution)/shard_map/all_gather | solution.py:12
  17.2 5.0 %copy-start.14 = (s32[9]{0:T(128)S(1)}, s32[9]{0:T(128)}, u32[]{:S(2)}) copy-start(s32[9]{0:T(128)} %param.17) | copy-start | bytes 112
  17.2 6.8 %slice-start = ((bf16[128,2,256]{2,1,0:T(2,128)(2,1)}), bf16[120,2,256]{2,1,0:T(2,128)(2,1)S(1)}, s32[]{:S(2)}) async-start(bf16[128,2,256]{2,1,0:T(2,128)(2,1)} %param.14), calls=%async_computation.6 | async-start | bytes 245760 | tf_op jit(solution)/shard_map/slice | solution.py:57
  25.2 3.9 %copy-start.1 = (bf16[1408,2,128]{2,1,0:T(2,128)(2,1)S(1)}, bf16[1408,2,128]{2,1,0:T(2,128)(2,1)}, u32[]{:S(2)}) copy-start(bf16[1408,2,128]{2,1,0:T(2,128)(2,1)} %reshape_reshape_squeeze.6) | copy-start | bytes 2162692
  40.8 6.5 %copy-start.12 = (f32[128]{0:T(128)S(1)}, f32[128]{0:T(128)}, u32[]{:S(2)}) copy-start(f32[128]{0:T(128)} %get-tuple-element.15) | copy-start | bytes 1540
  45.7 3.1 copy-start.11
  47.3 3.1 copy-start.10
  48.9 3.1 copy-start.9
  50.4 3.1 copy-start.8
  52.0 3.1 copy-start.7
  53.6 3.1 copy-start.6
  55.1 4.0 %copy-start.4 = (s32[16,2]{0,1:T(2,128)S(1)}, s32[16,2]{0,1:T(2,128)}, u32[]{:S(2)}) copy-start(s32[16,2]{0,1:T(2,128)} %param.22) | copy-start | bytes 388
  59.0 60.8 %copy-start.3 = (bf16[16,2048]{1,0:T(8,128)(2,1)S(1)}, bf16[16,2048]{1,0:T(8,128)(2,1)}, u32[]{:S(2)}) copy-start(bf16[16,2048]{1,0:T(8,128)(2,1)} %param.13) | copy-start | bytes 196612
  59.0 61.0 %copy-start.5 = (f32[2048]{0:T(1024)S(1)}, f32[2048]{0:T(1024)}, u32[]{:S(2)}) copy-start(f32[2048]{0:T(1024)} %param.21) | copy-start | bytes 24580
  59.1 131.4 %all-gather.4.cloned.1.call-start = ((), (), s32[]{:S(2)}) async-start(), calls=%async_computation.3 | async-start | bytes 8650752 | tf_op jit(solution)/shard_map/all_gather | solution.py:103
  120.0 78.0 %copy-start.2 = (bf16[16,2048]{1,0:T(8,128)(2,1)}, bf16[16,2048]{1,0:T(8,128)(2,1)S(1)}, u32[]{:S(2)}) copy-start(bf16[16,2048]{1,0:T(8,128)(2,1)S(1)} %get-tuple-element.19) | copy-start | bytes 196612
  136.4 174.1 %reduce-scatter.2.cloned.1.call-start = ((), (), s32[]{:S(2)}) async-start(), calls=%async_computation.4 | async-start | bytes 8650752 | tf_op jit(solution)/shard_map/reduce_scatter | solution.py:108
  210.6 107.1 %copy-start.13 = (f32[16,2]{0,1:T(2,128)S(1)}, f32[16,2]{0,1:T(2,128)}, u32[]{:S(2)}) copy-start(f32[16,2]{0,1:T(2,128)} %param.23) | copy-start | bytes 388
  310.5 17.5 %all-to-all-start.1 = ((bf16[8,8,2048]{2,1,0:T(8,128)(2,1)}), bf16[8,8,2048]{2,1,0:T(8,128)(2,1)S(1)}, u32[]{:S(2)}, u32[]{:S(2)}) async-start(bf16[8,8,2048]{2,1,0:T(8,128)(2,1)} %bitcast.103), calls=%async_computation.2 | async-start | bytes 524288 | tf_op jit(solution)/shard_map/all_to_all | solution.py:114
Sparse Core Ops, SparseCore 0:
  59.2 57.6 all-gather.5
  136.6 53.8 all-gather.3
  210.7 99.7 reduce-scatter.1
